TPU v7x, 32 devices: a whole 2x2x4 slice. The times are simulated.
32 devices in a mesh: dom: 8 (over y, x, core), rep: 4 (over z).
Axes of the slice: x: 2, y: 2, z: 4, core: 2. Of those that a mesh axis runs over, the one named last changes fastest.
Arguments:
- hop_feats: bfloat16 [3, 65536, 128], P(None, ('dom', 'rep')), may hold values from -6 to 6
- adj_local: bfloat16 [512, 12, 128, 128], P(('dom', 'rep')), may hold values from -0.125 to 0.125
- local_cols: int32 [512, 12], P(('dom', 'rep')), may hold values from 0 to 15
- adj_halo: bfloat16 [512, 4, 128, 128], P(('dom', 'rep')), may hold values from -0.125 to 0.125
- halo_cols: int32 [512, 4], P(('dom', 'rep')), may hold values from 0 to 3
- boundary_rows: int32 [32, 512], P(('dom', 'rep')), may hold values from 0 to 2047
- train_ids: int32 [32, 2048], P(('dom', 'rep')), may hold values from 0 to 2047, as said below
- shuffle: int32 [32, 2048], P(('dom', 'rep')), may hold values from 0 to 2047, as said below
- labels: int32 [65536], P(('dom', 'rep')), may hold values from 0 to 171
- labelled: int32 [65536], P(('dom', 'rep')), may hold values from 0 to 1
- w_first: bfloat16 [512, 1024], P(None, 'rep'), may hold values from -1 to 1
- w_second: bfloat16 [1024, 172], P('rep'), may hold values from -2 to 2
Outputs:
- next_hop: bfloat16 [65536, 128], P(('dom', 'rep'))
- batch_loss: float32 [32, 32], P(('dom', 'rep'))
- grad_first: float32 [512, 1024], P('dom', 'rep')
- grad_second: float32 [1024, 172], P('rep')
Inputs may be any that keep to these rules, and one draw needn't show every extreme that they name: `local_cols`: local tile indices of the partition's own row tiles. `halo_cols`: indices of received boundary tiles. `boundary_rows`: rows of the sending partition itself. `train_ids`: rows of the partition itself. `shuffle`: each row is a permutation of 0 .. 2047.
All inputs are finite; a program needn't handle non-finite values.
Results may differ from a plain program's by a relative error of at most 0.005.
The roundings to bfloat16 on the way count: a program that leaves them out, or rounds other values in their place, can miss the bound.
Values may be sent and summed in bfloat16 or wider, within the bound.
No kernel may reach another device: no remote copies, remote signals or barrier semaphores. Data moves between devices by JAX's collectives and lax.ppermute only.
A program may use at most 128 MiB of HBM per device.

v0:
```python
import jax
import jax.numpy as jnp
from jax import lax
from jax.sharding import PartitionSpec as P


def loss_head(logits, targets, weights_row):
    row_max = jnp.max(logits, axis=1, keepdims=True)
    expos = jnp.exp(logits - row_max)
    totals = jnp.sum(expos, axis=1, keepdims=True)
    classes = lax.broadcasted_iota(jnp.int32, logits.shape, 1)
    onehot = (classes == targets[:, None]).astype(jnp.float32)
    cross = jnp.log(totals[:, 0]) + row_max[:, 0] - jnp.sum(onehot * logits, axis=1)
    count = jnp.maximum(jnp.sum(weights_row), 1.0)
    dlogits = ((expos / totals - onehot) * (weights_row / count)[:, None]).astype(jnp.bfloat16)
    return (cross, dlogits)


def source_losses(cross, weights_row, groups):
    masks = weights_row.reshape(groups, -1)
    sums = jnp.sum(masks * cross.reshape(groups, -1), axis=1)
    return sums / jnp.maximum(jnp.sum(masks, axis=1), 1.0)


def batch_norm(pre):
    center = pre - jnp.mean(pre, axis=-2, keepdims=True)
    rstd = lax.rsqrt(jnp.mean(center * center, axis=-2, keepdims=True) + 1e-05)
    return (center * rstd, rstd)


def norm_back(grad, normed, rstd):
    mean_grad = jnp.mean(grad, axis=-2, keepdims=True)
    mean_proj = jnp.mean(grad * normed, axis=-2, keepdims=True)
    return (grad - mean_grad - normed * mean_proj) * rstd


def contract_rows(left, right):
    return lax.dot_general(
        left, right, (((0,), (0,)), ((), ())), preferred_element_type=jnp.float32
    )


def shards(
    hop_feats,
    adj_local,
    local_cols,
    adj_halo,
    halo_cols,
    boundary_rows,
    train_ids,
    shuffle,
    labels,
    labelled,
    w_first,
    w_second,
):
    num_dom = lax.axis_size("dom")
    num_rep = lax.axis_size("rep")
    devices = num_dom * num_rep
    tile = adj_local.shape[-1]
    row_tiles = adj_local.shape[0]
    rows = row_tiles * tile
    width = hop_feats.shape[2]
    hop_two = hop_feats[2]
    sent = jnp.take(hop_two, boundary_rows[0], axis=0)
    halo = lax.all_to_all(sent, ("dom", "rep"), split_axis=0, concat_axis=0, tiled=True)
    halo_count = halo.shape[0] // tile
    own_tiles = hop_two.reshape(row_tiles, tile, width)
    near = jnp.take(own_tiles, local_cols, axis=0)
    summed = jnp.einsum("ikab,ikbc->iac", adj_local, near, preferred_element_type=jnp.float32)
    far = jnp.take(halo.reshape(halo_count, tile, width), halo_cols, axis=0)
    summed = summed + jnp.einsum(
        "ikab,ikbc->iac", adj_halo, far, preferred_element_type=jnp.float32
    )
    next_hop = summed.reshape(rows, width).astype(jnp.bfloat16)
    order = jnp.take(train_ids[0], shuffle[0], axis=0)
    allfeat = jnp.concatenate([hop_feats[0], hop_feats[1], hop_two, next_hop], axis=1)
    feats = jnp.take(allfeat, order, axis=0)
    own_labels = jnp.take(labels, order, axis=0)
    own_marks = jnp.take(labelled, order, axis=0)
    target_pair = jnp.stack([own_labels, own_marks], axis=0)
    batch = lax.all_to_all(feats, ("dom", "rep"), split_axis=0, concat_axis=0, tiled=True)
    got_pair = lax.all_to_all(target_pair, ("dom", "rep"), split_axis=1, concat_axis=1, tiled=True)
    targets = got_pair[0]
    weights_row = got_pair[1].astype(jnp.float32)
    first_whole, second_whole = (
        lax.all_gather(w_first, "rep", axis=1, tiled=True),
        lax.all_gather(w_second, "rep", axis=0, tiled=True),
    )
    hidden_pre = jnp.dot(batch, first_whole, preferred_element_type=jnp.float32)
    normed, rstd = batch_norm(hidden_pre)
    hidden = jnp.maximum(normed, 0.0).astype(jnp.bfloat16)
    logits = jnp.dot(hidden, second_whole, preferred_element_type=jnp.float32)
    cross, dlogits = loss_head(logits, targets, weights_row)
    grad_two_full = contract_rows(hidden, dlogits)
    dhidden = lax.dot_general(
        dlogits, second_whole, (((1,), (1,)), ((), ())), preferred_element_type=jnp.float32
    )
    masked = jnp.where(normed > 0, dhidden, 0.0)
    dpre = norm_back(masked, normed, rstd).astype(jnp.bfloat16)
    grad_one_full = contract_rows(batch, dpre)
    grad_one_rep, grad_two_rep = (
        lax.psum_scatter(grad_one_full, "rep", scatter_dimension=1, tiled=True),
        lax.psum_scatter(grad_two_full, "rep", scatter_dimension=0, tiled=True),
    )
    grad_one = lax.psum_scatter(grad_one_rep, "dom", scatter_dimension=0, tiled=True)
    grad_two = lax.psum(grad_two_rep, "dom")
    loss = source_losses(cross, weights_row, devices)
    return (next_hop, loss.reshape(1, devices), grad_one, grad_two)


def solution(mesh):
    placed = (
        P(None, ("dom", "rep"), None),
        P(("dom", "rep"), None, None, None),
        P(("dom", "rep"), None),
        P(("dom", "rep"), None, None, None),
        P(("dom", "rep"), None),
        P(("dom", "rep"), None),
        P(("dom", "rep"), None),
        P(("dom", "rep"), None),
        P(("dom", "rep")),
        P(("dom", "rep")),
        P(None, "rep"),
        P("rep", None),
    )
    return jax.shard_map(
        shards,
        mesh=mesh,
        in_specs=placed,
        out_specs=(
            P(("dom", "rep"), None),
            P(("dom", "rep"), None),
            P("dom", "rep"),
            P("rep", None),
        ),
        check_vma=False,
    )
```

profile of v0, /device:TPU:0, one launch (start us, length us, event | category | flops | bytes accessed | tf_op | source)
XLA Modules:
  0.0 375.0 jit_solution(16362593156664925678)
XLA Ops:
  7.2 0.8 compare_select_fusion.5
  8.0 0.5 broadcast.147
  8.5 1.3 reduce.13
  9.9 0.1 squeeze.21
  10.0 2.6 slice_bitcast_fusion.1
  12.7 1.3 gather_fusion.1
  14.0 0.8 broadcast_select_fusion.1
  14.8 7.3 %all-to-all-start = ((bf16[32,16,128]{2,1,0:T(8,128)(2,1)}), bf16[32,16,128]{2,1,0:T(8,128)(2,1)S(1)}, u32[]{:S(2)}, u32[]{:S(2)}) async-start(bf16[32,16,128]{2,1,0:T(8,128)(2,1)} %broadcast_select_fusion.1), calls=%async_computation | async-start | bytes 262144 | tf_op jit(solution)/shard_map/all_to_all | solution.py:66
  22.2 0.1 copy.21
  22.2 0.1 reshape.202
  22.4 11.8 %gather_fusion.4 = s32[2048]{0:T(1024)S(1)} fusion(s32[2048]{0:T(1024)S(1)} %bitcast.44, s32[2048]{0:T(1024)S(1)} %fusion.25), kind=kCustom, calls=%fused_computation.clone | custom fusion | bytes 24576 | tf_op jit(solution)/shard_map/jit(_take)/gather | solution.py:76
  34.2 0.7 copy-done.2
  34.9 11.8 %gather_fusion.6 = s32[2048]{0:T(1024)S(1)} fusion(s32[2048]{0:T(1024)S(1)} %copy-done.2, s32[2048]{0:T(1024)S(1)} %broadcast_clamp_fusion), kind=kCustom, calls=%fused_computation.2.clone | custom fusion | bytes 24576 | tf_op jit(solution)/shard_map/jit(_take)/gather | solution.py:80
  46.7 11.8 %gather_fusion.5 = s32[2048]{0:T(1024)S(1)} fusion(s32[2048]{0:T(1024)S(1)} %copy-done.3, s32[2048]{0:T(1024)S(1)} %broadcast_clamp_fusion), kind=kCustom, calls=%fused_computation.1.clone | custom fusion | bytes 24576 | tf_op jit(solution)/shard_map/jit(_take)/gather | solution.py:79
  58.5 0.1 stack.10
  58.6 0.1 stack.9
  58.7 0.1 reshape.186
  58.8 0.1 broadcast_in_dim.71
  58.9 0.1 copy.20
  59.0 0.7 reshape.253
  59.7 8.0 %gather_fusion = bf16[192,128,128]{2,1,0:T(8,128)(2,1)} fusion(bf16[16,128,128]{2,1,0:T(8,128)(2,1)S(1)} %bitcast.45, s32[1024]{0:T(1024)S(1)} %pad_clamp_fusion.2), kind=kCustom, calls=%fused_computation.3 | custom fusion | bytes 12583680 | tf_op jit(solution)/shard_map/jit(_take)/gather | solution.py:69
  67.7 5.8 %all-to-all-start.1 = ((s32[32,1,128]{2,1,0:T(1,128)}), s32[32,1,128]{2,1,0:T(1,128)S(1)}, u32[]{:S(2)}, u32[]{:S(2)}) async-start(s32[32,1,128]{2,1,0:T(1,128)} %reshape.253), calls=%async_computation.1 | async-start | bytes 32768 | tf_op jit(solution)/shard_map/all_to_all | solution.py:83
  73.6 2.2 gather_fusion.2
  75.8 2.4 fusion.9
  78.2 6.6 %fusion.18 = bf16[16,128,128]{1,2,0:T(8,128)(2,1)S(1)} fusion(f32[16,128,128]{1,2,0:T(8,128)S(1)} %fusion.9, bf16[16,12,128,128]{3,2,1,0:T(8,128)(2,1)} %param.15, bf16[16,12,128,128]{3,2,1,0:T(8,128)(2,1)} %bitcast.48, pred[16,12]{1,0:T(8,128)(4,1)S(1)} %compare_and_fusion.2), kind=kOutput, calls=%fused_computation.31 | convolution fusion | flops 808976384 | bytes 14155968 | tf_op jit(solution)/shard_map/ikab,ikbc->iac/dot_general | solution.py:70
  84.7 0.8 copy-done.8
  85.5 1.6 pad_maximum_fusion
  87.1 11.1 %gather_fusion.3 = bf16[2048,512]{1,0:T(8,128)(2,1)} fusion(bf16[2048,512]{1,0:T(8,128)(2,1)} %pad_maximum_fusion, s32[2048]{0:T(1024)S(1)} %broadcast_clamp_fusion), kind=kCustom, calls=%fused_computation.6 | custom fusion | bytes 4202496 | tf_op jit(solution)/shard_map/jit(_take)/gather | solution.py:78
  98.2 2.8 broadcast_select_fusion
  101.0 6.0 %all-to-all-start.2 = ((bf16[32,64,512]{2,1,0:T(8,128)(2,1)}), bf16[32,64,512]{2,1,0:T(8,128)(2,1)}, u32[]{:S(2)}, u32[]{:S(2)}) async-start(bf16[32,64,512]{2,1,0:T(8,128)(2,1)} %broadcast_select_fusion), calls=%async_computation.2 | async-start | bytes 4194304 | tf_op jit(solution)/shard_map/all_to_all | solution.py:82
  107.0 0.0 all-gather.2.cloned.1.call-start
  107.0 0.7 all-gather.2.cloned.1.call-update
  107.7 0.0 reduce-scatter.8.cloned.1.call-start
  107.7 73.9 %all_gather.7 = bf16[1024,172]{0,1:T(8,128)(2,1)} all-gather(bf16[256,172]{0,1:T(8,128)(2,1)S(1)} %copy-done.9), channel_id=1, replica_groups=mesh['dom'=8,'rep'=4] {'rep'}, dimensions={0}, use_global_device_ids=true | all-gather | bytes 440320 | tf_op jit(solution)/shard_map/all_gather | solution.py:88
  181.7 0.5 broadcast.150
  182.2 0.7 reduce.14
  182.9 0.1 reshape.254
  183.0 0.6 fusion.32
  184.3 0.8 divide_reduce_fusion
  185.1 0.7 div.54
  185.8 0.6 slice_reduce_fusion
  186.4 0.7 eq.10
  187.1 4.2 %fusion.35 = (f32[1024]{0:T(1024)S(1)}, f32[2048,1024]{1,0:T(8,128)S(1)}) fusion(bf16[2048,512]{1,0:T(8,128)(2,1)} %bitcast.21, bf16[512,1024]{1,0:T(8,128)(2,1)} %all-gather.2.cloned.1.call-done), kind=kOutput, calls=%fused_computation.77 | convolution fusion | flops 2149579776 | bytes 11538432 | tf_op jit(solution)/shard_map/dot_general | solution.py:90
  191.3 0.9 multiply_reduce_fusion.1
  192.2 0.3 copy-done.7
  192.6 1.6 fusion.36
  194.2 1.0 fusion.21
  195.2 0.6 copy-done.13
  195.8 2.5 fusion.23
  198.3 7.4 %fusion = (f32[1024]{0:T(1024)}, f32[1024]{0:T(1024)}, f32[2048,1024]{1,0:T(8,128)}) fusion(f32[2048,1024]{1,0:T(8,128)} %copy-done.4, f32[1024]{0:T(1024)S(1)} %add_rsqrt_fusion, f32[1024]{0:T(1024)S(1)} %broadcast_multiply_fusion.2, bf16[1024,172]{0,1:T(8,128)(2,1)} %all_gather.7, f32[2048,172]{0,1:T(8,128)S(1)} %get-tuple-element.22, f32[2048]{0:T(1024)} %div.54, ...), kind=kOutput, calls=%fused_computation.13 | convolution fusion | flops 738564096 | bytes 18587648 | tf_op jit(solution)/shard_map/dot_general | solution.py:96
  205.7 0.0 reduce-scatter.4.cloned.1.call-start
  205.8 0.7 broadcast_multiply_fusion
  206.5 10.6 %fusion.4 = f32[512,1024]{1,0:T(8,128)} fusion(bf16[2048,512]{1,0:T(8,128)(2,1)} %bitcast.21, f32[2048,1024]{1,0:T(8,128)} %get-tuple-element.23, f32[2048,1024]{1,0:T(8,128)} %copy-done.4, f32[1024]{0:T(1024)S(1)} %get-tuple-element.24, f32[1024]{0:T(1024)S(1)} %get-tuple-element.25, f32[1024]{0:T(1024)S(1)} %add_rsqrt_fusion, ...), kind=kOutput, calls=%fused_computation.17 | convolution fusion | flops 2166358016 | bytes 20987904 | tf_op jit(solution)/shard_map/dot_general | solution.py:38
  217.1 0.0 reduce-scatter.4.cloned.1.call-update
  217.1 0.0 all-reduce.2.cloned.1.call-start
  217.2 11.8 %reduce-scatter.8.cloned.1.call-done = f32[256,172]{0,1:T(8,128)} async-done(((f32[1024,172]{0,1:T(8,128)}), f32[256,172]{0,1:T(8,128)}) %reduce-scatter.8.cloned.1.call-update) | async-done | bytes 176144 | tf_op jit(solution)/shard_map/reduce_scatter | solution.py:104
  229.0 0.0 reduce-scatter.6.cloned.1.call-start
  229.0 44.9 %reduce-scatter.4.cloned.1.call-done = f32[512,256]{1,0:T(8,128)} async-done(((f32[512,1024]{1,0:T(8,128)}), f32[512,256]{1,0:T(8,128)}) %reduce-scatter.4.cloned.1.call-update) | async-done | bytes 524304 | tf_op jit(solution)/shard_map/reduce_scatter | solution.py:103
  274.0 0.1 sub.43
  274.1 0.1 multiply_reduce_fusion.2
  274.2 0.5 fusion.26
  274.7 54.4 %all-reduce.2.cloned.1.call-done = f32[256,172]{0,1:T(8,128)} async-done(((f32[256,172]{0,1:T(8,128)}), f32[256,172]{0,1:T(8,128)}) %all-reduce.2.cloned.1.call-update) | async-done | bytes 176144 | tf_op jit(solution)/shard_map/psum | solution.py:107
  329.2 37.7 %reduce-scatter.6.cloned.1.call-done = f32[64,256]{1,0:T(8,128)} async-done(((f32[512,256]{1,0:T(8,128)}), f32[64,256]{1,0:T(8,128)}) %reduce-scatter.6.cloned.1.call-update) | async-done | bytes 65552 | tf_op jit(solution)/shard_map/reduce_scatter | solution.py:106
  366.9 1.6 copy.25
  (59 shorter events, 0.3 us)
Async XLA Ops:
  7.2 68.6 %copy-start = (bf16[16,4,128,128]{3,2,1,0:T(8,128)(2,1)S(1)}, bf16[16,4,128,128]{3,2,1,0:T(8,128)(2,1)}, u32[]{:S(2)}) copy-start(bf16[16,4,128,128]{3,2,1,0:T(8,128)(2,1)} %param.17) | copy-start | bytes 6291460
  10.0 12.1 %copy-start.18 = (s32[16,4]{0,1:T(4,128)S(1)}, s32[16,4]{0,1:T(4,128)}, u32[]{:S(2)}) copy-start(s32[16,4]{0,1:T(4,128)} %param.18) | copy-start | bytes 772
  10.0 12.4 %copy-start.10 = (s32[1,2048]{1,0:T(1,128)S(1)}, s32[1,2048]{1,0:T(1,128)}, u32[]{:S(2)}) copy-start(s32[1,2048]{1,0:T(1,128)} %param.21) | copy-start | bytes 24580
  10.0 12.4 %copy-start.1 = (s32[1,2048]{1,0:T(1,128)S(1)}, s32[1,2048]{1,0:T(1,128)}, u32[]{:S(2)}) copy-start(s32[1,2048]{1,0:T(1,128)} %param.20) | copy-start | bytes 24580
  14.8 53.0 %all-to-all-start = ((bf16[32,16,128]{2,1,0:T(8,128)(2,1)}), bf16[32,16,128]{2,1,0:T(8,128)(2,1)S(1)}, u32[]{:S(2)}, u32[]{:S(2)}) async-start(bf16[32,16,128]{2,1,0:T(8,128)(2,1)} %broadcast_select_fusion.1), calls=%async_computation | async-start | bytes 262144 | tf_op jit(solution)/shard_map/all_to_all | solution.py:66
  34.2 0.7 copy-start.2
  34.9 11.8 %copy-start.3 = (s32[2048]{0:T(1024)S(1)}, s32[2048]{0:T(1024)}, u32[]{:S(2)}) copy-start(s32[2048]{0:T(1024)} %param.22) | copy-start | bytes 24580
  46.7 12.0 %copy-start.16 = (s32[16,12]{1,0:T(8,128)S(1)}, s32[16,12]{1,0:T(8,128)}, u32[]{:S(2)}) copy-start(s32[16,12]{1,0:T(8,128)} %param.16) | copy-start | bytes 2308
  67.7 33.2 %all-to-all-start.1 = ((s32[32,1,128]{2,1,0:T(1,128)}), s32[32,1,128]{2,1,0:T(1,128)S(1)}, u32[]{:S(2)}, u32[]{:S(2)}) async-start(s32[32,1,128]{2,1,0:T(1,128)} %reshape.253), calls=%async_computation.1 | async-start | bytes 32768 | tf_op jit(solution)/shard_map/all_to_all | solution.py:83
  78.1 7.4 %copy-start.5 = (bf16[2048,128]{1,0:T(8,128)(2,1)S(1)}, bf16[2048,128]{1,0:T(8,128)(2,1)}, u32[]{:S(2)}) copy-start(bf16[2048,128]{1,0:T(8,128)(2,1)} %get-tuple-element.13) | copy-start | bytes 1572868
  78.1 7.4 %copy-start.6 = (bf16[2048,128]{1,0:T(8,128)(2,1)S(1)}, bf16[2048,128]{1,0:T(8,128)(2,1)}, u32[]{:S(2)}) copy-start(bf16[2048,128]{1,0:T(8,128)(2,1)} %get-tuple-element.16) | copy-start | bytes 1572868
  84.7 0.8 copy-start.8
  101.0 6.8 %copy-start.9 = (bf16[256,172]{0,1:T(8,128)(2,1)S(1)}, bf16[256,172]{0,1:T(8,128)(2,1)}, u32[]{:S(2)}) copy-start(bf16[256,172]{0,1:T(8,128)(2,1)} %param.25) | copy-start | bytes 264196
  101.0 86.1 %all-to-all-start.2 = ((bf16[32,64,512]{2,1,0:T(8,128)(2,1)}), bf16[32,64,512]{2,1,0:T(8,128)(2,1)}, u32[]{:S(2)}, u32[]{:S(2)}) async-start(bf16[32,64,512]{2,1,0:T(8,128)(2,1)} %broadcast_select_fusion), calls=%async_computation.2 | async-start | bytes 4194304 | tf_op jit(solution)/shard_map/all_to_all | solution.py:82
  107.0 80.1 %all-gather.2.cloned.1.call-start = ((), (), s32[]{:S(2)}) async-start(), calls=%async_computation.6 | async-start | bytes 1310720 | tf_op jit(solution)/shard_map/all_gather | solution.py:87
  107.7 121.3 %reduce-scatter.8.cloned.1.call-start = ((), (), s32[]{:S(2)}) async-start(), calls=%async_computation.9 | async-start | bytes 901120 | tf_op jit(solution)/shard_map/reduce_scatter | solution.py:104
  191.3 3.9 %copy-start.4 = (f32[2048,1024]{1,0:T(8,128)}, f32[2048,1024]{1,0:T(8,128)S(1)}, u32[]{:S(2)}) copy-start(f32[2048,1024]{1,0:T(8,128)S(1)} %get-tuple-element.20) | copy-start | bytes 25165828
  191.3 1.3 copy-start.7
  192.6 1.6 copy-start.12
  192.6 3.2 copy-start.17
  195.2 0.6 copy-start.13
  205.7 68.2 %reduce-scatter.4.cloned.1.call-start = ((), (), s32[]{:S(2)}) async-start(), calls=%async_computation.7 | async-start | bytes 2621440 | tf_op jit(solution)/shard_map/reduce_scatter | solution.py:103
  217.1 56.9 %copy-start.14 = (f32[2048]{0:T(1024)S(1)}, f32[2048]{0:T(1024)}, u32[]{:S(2)}) copy-start(f32[2048]{0:T(1024)} %copy-done.13) | copy-start | bytes 24580
  217.1 56.9 %copy-start.15 = (f32[2048]{0:T(1024)S(1)}, f32[2048]{0:T(1024)}, u32[]{:S(2)}) copy-start(f32[2048]{0:T(1024)} %get-tuple-element.8) | copy-start | bytes 24580
  217.1 57.0 %copy-start.11 = (f32[1,32,64]{2,0,1:T(1,128)S(1)}, f32[1,32,64]{2,0,1:T(1,128)}, u32[]{:S(2)}) copy-start(f32[1,32,64]{2,0,1:T(1,128)} %get-tuple-element.18) | copy-start | bytes 24580
  217.1 57.1 %copy-start.19 = (f32[32]{0:T(128)S(1)}, f32[32]{0:T(128)}, u32[]{:S(2)}) copy-start(f32[32]{0:T(128)} %get-tuple-element.10) | copy-start | bytes 388
  217.1 112.0 %all-reduce.2.cloned.1.call-start = ((), (), s32[]{:S(2)}) async-start(), calls=%async_computation.10 | async-start | bytes 360448 | tf_op jit(solution)/shard_map/psum | solution.py:107
  229.0 137.9 %reduce-scatter.6.cloned.1.call-start = ((), (), s32[]{:S(2)}) async-start(), calls=%async_computation.8 | async-start | bytes 589824 | tf_op jit(solution)/shard_map/reduce_scatter | solution.py:106
Sparse Core Ops, SparseCore 0:
  109.3 55.8 all-gather.1
  205.8 23.0 reduce-scatter.7
  231.2 42.6 reduce-scatter.3
  276.9 52.1 all-reduce.1
  332.6 34.2 reduce-scatter.5
where the time goes:
time: 376 us; the launch traced here: 375 us
  waiting for transfers between devices  150 us (40%)
  blocking collectives  73.9 us (20%)
  local copies, waits for them, and re-layouts  68.5 us (18%)
  matrix products  35.3 us (9%)
  starting transfers between devices  19.3 us (5%)
  between operations  14.8 us (4%)
  other arithmetic  13.5 us (4%)
    all_gather x1, blocking collectives, shards(): lax.all_gather(w_second, 'rep', axis=0, tiled=True)  73.9 us
    psum x1, waiting for transfers between devices, shards(): grad_two = lax.psum(grad_two_rep, 'dom')  54.4 us
    reduce_scatter x1, waiting for transfers between devices, shards(): lax.psum_scatter(grad_one_full, 'rep', scatter_dimension=1, tiled=True)  44.9 us
    reduce_scatter x1, waiting for transfers between devices, shards(): lax.psum_scatter(grad_one_rep, 'dom', scatter_dimension=0, tiled=True)  37.7 us
    dot_general x2, matrix products, contract_rows(): lax.dot_general(left, right, (((0,), (0,)), ((), ())), preferred_element_...  13.2 us
    gather x1, local copies, waits for them, and re-layouts, shards(): order = jnp.take(train_ids[0], shuffle[0], axis=0)  11.8 us
    gather x1, local copies, waits for them, and re-layouts, shards(): own_labels = jnp.take(labels, order, axis=0)  11.8 us
    gather x1, local copies, waits for them, and re-layouts, shards(): own_marks = jnp.take(labelled, order, axis=0)  11.8 us
  transfers between devices with their start and end apart: 8, of which 4 were waited for; matrix products, arithmetic and copies ran while one was open for 23% of the time, Pallas kernels for 0%

commit v1 on v0

--- a/solution.py
+++ b/solution.py
@@ -104,7 +104,11 @@
         lax.psum_scatter(grad_two_full, "rep", scatter_dimension=0, tiled=True),
     )
     grad_one = lax.psum_scatter(grad_one_rep, "dom", scatter_dimension=0, tiled=True)
-    grad_two = lax.psum(grad_two_rep, "dom")
+    nodes = lax.psum(1, "dom")
+    grad_two = grad_two_rep
+    for c in [[(h, h ^ t) for h in range(nodes)] for t in (1, 2, 4, 8, 16) if t < nodes]:
+        now = lax.ppermute(grad_two, "dom", c)
+        grad_two = grad_two + now
     loss = source_losses(cross, weights_row, devices)
     return (next_hop, loss.reshape(1, devices), grad_one, grad_two)
 

time: 376 us -> 316 us (0.84)
  waiting for transfers between devices: 150 us -> 93 us
  matrix products: 35.3 us -> 29.5 us
    psum x1 -> x0, waiting for transfers between devices: 54.4 us -> none  [shards(): grad_two = lax.psum(grad_two_rep, 'dom')]
    reduce_scatter x1, waiting for transfers between devices: 37.7 us -> 20.9 us  [shards(): lax.psum_scatter(grad_one_rep, 'dom', scatter_dimension=0, tiled=True)]
    reduce_scatter x1, waiting for transfers between devices: 11.8 us -> 24.5 us  [shards(): lax.psum_scatter(grad_two_full, 'rep', scatter_dimension=0, tiled=True)]
    ppermute x0 -> x3, waiting for transfers between devices: none -> 8.96 us  [shards(): now = lax.ppermute(grad_two, 'dom', c)]
    reduce_scatter x1, waiting for transfers between devices: 44.9 us -> 37.9 us  [shards(): lax.psum_scatter(grad_one_full, 'rep', scatter_dimension=1, tiled=True)]
    dot_general x1, matrix products: 7.41 us -> 2.74 us  [shards(): lax.dot_general(dlogits, second_whole, (((1,), (1,)), ((), ())), preferre...]
  transfers between devices with their start and end apart: 8 -> 10, of which waited for: 4 -> 6; matrix products, arithmetic and copies ran while one was open for 23% -> 27% of each run, Pallas kernels for 0% -> 0%
where the time goes in v1:
time: 316 us
  waiting for transfers between devices  93 us (29%)
  blocking collectives  73.9 us (23%)
  local copies, waits for them, and re-layouts  66.3 us (21%)
  matrix products  29.5 us (9%)
  starting transfers between devices  22.3 us (7%)
  other arithmetic  15.9 us (5%)
  between operations  14.8 us (5%)
    all_gather x1, blocking collectives, shards(): lax.all_gather(w_second, 'rep', axis=0, tiled=True)  73.9 us
    reduce_scatter x1, waiting for transfers between devices, shards(): lax.psum_scatter(grad_one_full, 'rep', scatter_dimension=1, tiled=True)  37.9 us
    reduce_scatter x1, waiting for transfers between devices, shards(): lax.psum_scatter(grad_two_full, 'rep', scatter_dimension=0, tiled=True)  24.5 us
    reduce_scatter x1, waiting for transfers between devices, shards(): lax.psum_scatter(grad_one_rep, 'dom', scatter_dimension=0, tiled=True)  20.9 us
    dot_general x2, matrix products, contract_rows(): lax.dot_general(left, right, (((0,), (0,)), ((), ())), preferred_element_...  12 us
    gather x1, local copies, waits for them, and re-layouts, shards(): order = jnp.take(train_ids[0], shuffle[0], axis=0)  11.8 us
    gather x1, local copies, waits for them, and re-layouts, shards(): own_labels = jnp.take(labels, order, axis=0)  11.8 us
    gather x1, local copies, waits for them, and re-layouts, shards(): own_marks = jnp.take(labelled, order, axis=0)  11.8 us
  transfers between devices with their start and end apart: 10, of which 6 were waited for; matrix products, arithmetic and copies ran while one was open for 27% of the time, Pallas kernels for 0%

profile of v1, /device:TPU:0, one launch (start us, length us, event | category | flops | bytes accessed | tf_op | source)
XLA Modules:
  0.0 315.7 jit_solution(13284734405977911383)
XLA Ops:
  7.2 0.8 compare_select_fusion.5
  8.0 0.5 broadcast.147
  8.5 1.3 reduce.13
  9.9 0.1 squeeze.21
  10.0 2.6 slice_bitcast_fusion.1
  12.7 1.3 gather_fusion.1
  14.0 0.8 broadcast_select_fusion.1
  14.8 7.3 %all-to-all-start = ((bf16[32,16,128]{2,1,0:T(8,128)(2,1)}), bf16[32,16,128]{2,1,0:T(8,128)(2,1)S(1)}, u32[]{:S(2)}, u32[]{:S(2)}) async-start(bf16[32,16,128]{2,1,0:T(8,128)(2,1)} %broadcast_select_fusion.1), calls=%async_computation | async-start | bytes 262144 | tf_op jit(solution)/shard_map/all_to_all | solution.py:66
  22.2 0.1 copy.21
  22.2 0.1 reshape.202
  22.4 11.8 %gather_fusion.4 = s32[2048]{0:T(1024)S(1)} fusion(s32[2048]{0:T(1024)S(1)} %bitcast.44, s32[2048]{0:T(1024)S(1)} %fusion.25), kind=kCustom, calls=%fused_computation.clone | custom fusion | bytes 24576 | tf_op jit(solution)/shard_map/jit(_take)/gather | solution.py:76
  34.2 0.7 copy-done.2
  34.9 11.8 %gather_fusion.6 = s32[2048]{0:T(1024)S(1)} fusion(s32[2048]{0:T(1024)S(1)} %copy-done.2, s32[2048]{0:T(1024)S(1)} %broadcast_clamp_fusion), kind=kCustom, calls=%fused_computation.2.clone | custom fusion | bytes 24576 | tf_op jit(solution)/shard_map/jit(_take)/gather | solution.py:80
  46.7 11.8 %gather_fusion.5 = s32[2048]{0:T(1024)S(1)} fusion(s32[2048]{0:T(1024)S(1)} %copy-done.3, s32[2048]{0:T(1024)S(1)} %broadcast_clamp_fusion), kind=kCustom, calls=%fused_computation.1.clone | custom fusion | bytes 24576 | tf_op jit(solution)/shard_map/jit(_take)/gather | solution.py:79
  58.5 0.1 stack.10
  58.6 0.1 stack.9
  58.7 0.1 reshape.186
  58.8 0.1 broadcast_in_dim.71
  58.9 0.1 copy.20
  59.0 0.7 reshape.253
  59.7 8.0 %gather_fusion = bf16[192,128,128]{2,1,0:T(8,128)(2,1)} fusion(bf16[16,128,128]{2,1,0:T(8,128)(2,1)S(1)} %bitcast.45, s32[1024]{0:T(1024)S(1)} %pad_clamp_fusion.2), kind=kCustom, calls=%fused_computation.3 | custom fusion | bytes 12583680 | tf_op jit(solution)/shard_map/jit(_take)/gather | solution.py:69
  67.7 5.8 %all-to-all-start.1 = ((s32[32,1,128]{2,1,0:T(1,128)}), s32[32,1,128]{2,1,0:T(1,128)S(1)}, u32[]{:S(2)}, u32[]{:S(2)}) async-start(s32[32,1,128]{2,1,0:T(1,128)} %reshape.253), calls=%async_computation.1 | async-start | bytes 32768 | tf_op jit(solution)/shard_map/all_to_all | solution.py:83
  73.6 2.2 gather_fusion.2
  75.8 2.4 fusion.9
  78.2 6.6 %fusion.18 = bf16[16,128,128]{1,2,0:T(8,128)(2,1)S(1)} fusion(f32[16,128,128]{1,2,0:T(8,128)S(1)} %fusion.9, bf16[16,12,128,128]{3,2,1,0:T(8,128)(2,1)} %param.15, bf16[16,12,128,128]{3,2,1,0:T(8,128)(2,1)} %bitcast.48, pred[16,12]{1,0:T(8,128)(4,1)S(1)} %compare_and_fusion.2), kind=kOutput, calls=%fused_computation.31 | convolution fusion | flops 808976384 | bytes 14155968 | tf_op jit(solution)/shard_map/ikab,ikbc->iac/dot_general | solution.py:70
  84.7 0.8 copy-done.8
  85.5 1.6 pad_maximum_fusion
  87.1 11.1 %gather_fusion.3 = bf16[2048,512]{1,0:T(8,128)(2,1)} fusion(bf16[2048,512]{1,0:T(8,128)(2,1)} %pad_maximum_fusion, s32[2048]{0:T(1024)S(1)} %broadcast_clamp_fusion), kind=kCustom, calls=%fused_computation.6 | custom fusion | bytes 4202496 | tf_op jit(solution)/shard_map/jit(_take)/gather | solution.py:78
  98.2 2.8 broadcast_select_fusion
  101.0 6.0 %all-to-all-start.2 = ((bf16[32,64,512]{2,1,0:T(8,128)(2,1)}), bf16[32,64,512]{2,1,0:T(8,128)(2,1)}, u32[]{:S(2)}, u32[]{:S(2)}) async-start(bf16[32,64,512]{2,1,0:T(8,128)(2,1)} %broadcast_select_fusion), calls=%async_computation.2 | async-start | bytes 4194304 | tf_op jit(solution)/shard_map/all_to_all | solution.py:82
  107.0 0.7 all-gather.2.cloned.1.call-update
  107.7 73.9 %all_gather.7 = bf16[1024,172]{0,1:T(8,128)(2,1)} all-gather(bf16[256,172]{0,1:T(8,128)(2,1)S(1)} %copy-done.9), channel_id=1, replica_groups=mesh['dom'=8,'rep'=4] {'rep'}, dimensions={0}, use_global_device_ids=true | all-gather | bytes 440320 | tf_op jit(solution)/shard_map/all_gather | solution.py:88
  181.7 0.5 broadcast.150
  182.2 0.7 reduce.14
  182.9 0.1 reshape.254
  183.0 0.6 fusion.32
  184.3 0.8 divide_reduce_fusion
  185.1 0.7 div.54
  185.8 0.6 slice_reduce_fusion
  186.4 0.7 eq.10
  187.1 4.3 %fusion.35 = (f32[1024]{0:T(1024)S(1)}, f32[2048,1024]{1,0:T(8,128)S(1)}) fusion(bf16[2048,512]{1,0:T(8,128)(2,1)} %bitcast.21, bf16[512,1024]{1,0:T(8,128)(2,1)} %all-gather.2.cloned.1.call-done), kind=kOutput, calls=%fused_computation.77 | convolution fusion | flops 2149579776 | bytes 11538432 | tf_op jit(solution)/shard_map/dot_general | solution.py:90
  191.4 0.9 multiply_reduce_fusion.1
  192.3 0.3 copy-done.7
  192.6 1.6 fusion.36
  194.3 1.0 fusion.21
  195.2 2.7 fusion
  198.0 6.0 %fusion.4 = f32[512,1024]{1,0:T(8,128)} fusion(bf16[2048,512]{1,0:T(8,128)(2,1)} %bitcast.21, f32[2048,1024]{1,0:T(8,128)S(1)} %get-tuple-element.23, f32[2048,1024]{1,0:T(8,128)S(1)} %get-tuple-element.20, f32[1024]{0:T(1024)S(1)} %get-tuple-element.24, f32[1024]{0:T(1024)S(1)} %get-tuple-element.25, f32[1024]{0:T(1024)S(1)} %add_rsqrt_fusion, ...), kind=kOutput, calls=%fused_computation.17 | convolution fusion | flops 2166358016 | bytes 20987904 | tf_op jit(solution)/shard_map/dot_general | solution.py:38
  204.1 0.0 reduce-scatter.8.cloned.1.call-start
  204.1 6.0 %fusion.23 = f32[1024,172]{0,1:T(8,128)} fusion(f32[2048,1024]{1,0:T(8,128)} %copy-done.4, f32[1024]{0:T(1024)S(1)} %add_rsqrt_fusion, f32[1024]{0:T(1024)S(1)} %broadcast_multiply_fusion.2, f32[2048,172]{0,1:T(8,128)S(1)} %get-tuple-element.22, f32[2048]{0:T(1024)} %div.54, f32[2048]{0:T(1024)} %copy-done.12, s32[2048]{0:T(1024)} %eq.10, ...), kind=kOutput, calls=%fused_computation.34 | convolution fusion | flops 732274688 | bytes 10543104 | tf_op jit(solution)/shard_map/dot_general | solution.py:38
  210.1 0.0 reduce-scatter.6.cloned.1.call-start
  210.2 37.9 %reduce-scatter.4.cloned.1.call-done = f32[512,256]{1,0:T(8,128)} async-done(((f32[512,1024]{1,0:T(8,128)}), f32[512,256]{1,0:T(8,128)}) %reduce-scatter.4.cloned.1.call-update) | async-done | bytes 524304 | tf_op jit(solution)/shard_map/reduce_scatter | solution.py:103
  248.0 24.5 %reduce-scatter.8.cloned.1.call-done = f32[256,172]{0,1:T(8,128)} async-done(((f32[1024,172]{0,1:T(8,128)}), f32[256,172]{0,1:T(8,128)}) %reduce-scatter.8.cloned.1.call-update) | async-done | bytes 176144 | tf_op jit(solution)/shard_map/reduce_scatter | solution.py:104
  272.6 1.6 collective-permute-done
  274.2 0.9 add.102
  275.2 1.5 collective-permute-start.1
  276.6 0.7 add_subtract_fusion
  277.4 0.1 sub.43
  277.4 0.8 multiply_reduce_fusion.2
  278.3 3.5 %collective-permute-done.1 = f32[256,172]{0,1:T(8,128)S(1)} collective-permute-done((f32[256,172]{0,1:T(8,128)S(1)}, f32[256,172]{0,1:T(8,128)S(1)}, u32[]{:S(2)}, u32[]{:S(2)}) %collective-permute-start.1) | collective-permute-done | bytes 176160 | tf_op jit(solution)/shard_map/ppermute | solution.py:110
  281.8 1.5 collective-permute-start.2
  283.3 0.5 fusion.26
  283.8 3.8 %collective-permute-done.2 = f32[256,172]{0,1:T(8,128)S(1)} collective-permute-done((f32[256,172]{0,1:T(8,128)S(1)}, f32[256,172]{0,1:T(8,128)S(1)}, u32[]{:S(2)}, u32[]{:S(2)}) %collective-permute-start.2) | collective-permute-done | bytes 176160 | tf_op jit(solution)/shard_map/ppermute | solution.py:110
  287.6 0.7 add.104
  288.3 20.9 %reduce-scatter.6.cloned.1.call-done = f32[64,256]{1,0:T(8,128)} async-done(((f32[512,256]{1,0:T(8,128)}), f32[64,256]{1,0:T(8,128)}) %reduce-scatter.6.cloned.1.call-update) | async-done | bytes 65552 | tf_op jit(solution)/shard_map/reduce_scatter | solution.py:106
  (58 shorter events, 0.4 us)
Async XLA Ops:
  7.2 68.6 %copy-start = (bf16[16,4,128,128]{3,2,1,0:T(8,128)(2,1)S(1)}, bf16[16,4,128,128]{3,2,1,0:T(8,128)(2,1)}, u32[]{:S(2)}) copy-start(bf16[16,4,128,128]{3,2,1,0:T(8,128)(2,1)} %param.17) | copy-start | bytes 6291460
  10.0 12.1 %copy-start.15 = (s32[16,4]{0,1:T(4,128)S(1)}, s32[16,4]{0,1:T(4,128)}, u32[]{:S(2)}) copy-start(s32[16,4]{0,1:T(4,128)} %param.18) | copy-start | bytes 772
  10.0 12.4 %copy-start.10 = (s32[1,2048]{1,0:T(1,128)S(1)}, s32[1,2048]{1,0:T(1,128)}, u32[]{:S(2)}) copy-start(s32[1,2048]{1,0:T(1,128)} %param.21) | copy-start | bytes 24580
  10.0 12.4 %copy-start.1 = (s32[1,2048]{1,0:T(1,128)S(1)}, s32[1,2048]{1,0:T(1,128)}, u32[]{:S(2)}) copy-start(s32[1,2048]{1,0:T(1,128)} %param.20) | copy-start | bytes 24580
  14.8 53.0 %all-to-all-start = ((bf16[32,16,128]{2,1,0:T(8,128)(2,1)}), bf16[32,16,128]{2,1,0:T(8,128)(2,1)S(1)}, u32[]{:S(2)}, u32[]{:S(2)}) async-start(bf16[32,16,128]{2,1,0:T(8,128)(2,1)} %broadcast_select_fusion.1), calls=%async_computation | async-start | bytes 262144 | tf_op jit(solution)/shard_map/all_to_all | solution.py:66
  34.2 0.7 copy-start.2
  34.9 11.8 %copy-start.3 = (s32[2048]{0:T(1024)S(1)}, s32[2048]{0:T(1024)}, u32[]{:S(2)}) copy-start(s32[2048]{0:T(1024)} %param.22) | copy-start | bytes 24580
  46.7 12.0 %copy-start.13 = (s32[16,12]{1,0:T(8,128)S(1)}, s32[16,12]{1,0:T(8,128)}, u32[]{:S(2)}) copy-start(s32[16,12]{1,0:T(8,128)} %param.16) | copy-start | bytes 2308
  67.7 33.2 %all-to-all-start.1 = ((s32[32,1,128]{2,1,0:T(1,128)}), s32[32,1,128]{2,1,0:T(1,128)S(1)}, u32[]{:S(2)}, u32[]{:S(2)}) async-start(s32[32,1,128]{2,1,0:T(1,128)} %reshape.253), calls=%async_computation.1 | async-start | bytes 32768 | tf_op jit(solution)/shard_map/all_to_all | solution.py:83
  78.1 7.4 %copy-start.5 = (bf16[2048,128]{1,0:T(8,128)(2,1)S(1)}, bf16[2048,128]{1,0:T(8,128)(2,1)}, u32[]{:S(2)}) copy-start(bf16[2048,128]{1,0:T(8,128)(2,1)} %get-tuple-element.13) | copy-start | bytes 1572868
  78.1 7.4 %copy-start.6 = (bf16[2048,128]{1,0:T(8,128)(2,1)S(1)}, bf16[2048,128]{1,0:T(8,128)(2,1)}, u32[]{:S(2)}) copy-start(bf16[2048,128]{1,0:T(8,128)(2,1)} %get-tuple-element.16) | copy-start | bytes 1572868
  84.7 0.8 copy-start.8
  101.0 6.8 %copy-start.9 = (bf16[256,172]{0,1:T(8,128)(2,1)S(1)}, bf16[256,172]{0,1:T(8,128)(2,1)}, u32[]{:S(2)}) copy-start(bf16[256,172]{0,1:T(8,128)(2,1)} %param.25) | copy-start | bytes 264196
  101.0 86.1 %all-to-all-start.2 = ((bf16[32,64,512]{2,1,0:T(8,128)(2,1)}), bf16[32,64,512]{2,1,0:T(8,128)(2,1)}, u32[]{:S(2)}, u32[]{:S(2)}) async-start(bf16[32,64,512]{2,1,0:T(8,128)(2,1)} %broadcast_select_fusion), calls=%async_computation.2 | async-start | bytes 4194304 | tf_op jit(solution)/shard_map/all_to_all | solution.py:82
  107.0 80.1 %all-gather.2.cloned.1.call-start = ((), (), s32[]{:S(2)}) async-start(), calls=%async_computation.6 | async-start | bytes 1310720 | tf_op jit(solution)/shard_map/all_gather | solution.py:87
  107.7 140.3 %reduce-scatter.4.cloned.1.call-start = ((), (), s32[]{:S(2)}) async-start(), calls=%async_computation.7 | async-start | bytes 2621440 | tf_op jit(solution)/shard_map/reduce_scatter | solution.py:103
  191.4 6.7 %copy-start.4 = (f32[2048,1024]{1,0:T(8,128)}, f32[2048,1024]{1,0:T(8,128)S(1)}, u32[]{:S(2)}) copy-start(f32[2048,1024]{1,0:T(8,128)S(1)} %get-tuple-element.20) | copy-start | bytes 25165828
  191.4 1.3 copy-start.7
  192.6 1.6 copy-start.11
  192.6 2.6 copy-start.14
  195.2 2.8 copy-start.12
  204.1 68.5 %reduce-scatter.8.cloned.1.call-start = ((), (), s32[]{:S(2)}) async-start(), calls=%async_computation.9 | async-start | bytes 901120 | tf_op jit(solution)/shard_map/reduce_scatter | solution.py:104
  210.1 73.3 %copy-start.16 = (f32[32]{0:T(128)S(1)}, f32[32]{0:T(128)}, u32[]{:S(2)}) copy-start(f32[32]{0:T(128)} %get-tuple-element.10) | copy-start | bytes 388
  210.1 99.1 %reduce-scatter.6.cloned.1.call-start = ((), (), s32[]{:S(2)}) async-start(), calls=%async_computation.8 | async-start | bytes 589824 | tf_op jit(solution)/shard_map/reduce_scatter | solution.py:106
  272.6 1.6 collective-permute-start
  275.2 6.7 %collective-permute-start.1 = (f32[256,172]{0,1:T(8,128)S(1)}, f32[256,172]{0,1:T(8,128)S(1)}, u32[]{:S(2)}, u32[]{:S(2)}) collective-permute-start(f32[256,172]{0,1:T(8,128)S(1)} %add.102), channel_id=1, source_target_pairs={{0,8},{4,12},{8,0},{12,4},{16,24},{20,28},{24,16},{28,20},{1,9},{5... | collective-permute-start | bytes 528392 | tf_op jit(solution)/shard_map/ppermute | solution.py:110
  281.8 5.8 %collective-permute-start.2 = (f32[256,172]{0,1:T(8,128)S(1)}, f32[256,172]{0,1:T(8,128)S(1)}, u32[]{:S(2)}, u32[]{:S(2)}) collective-permute-start(f32[256,172]{0,1:T(8,128)S(1)} %add.103), channel_id=1, source_target_pairs={{0,16},{4,20},{8,24},{12,28},{16,0},{20,4},{24,8},{28,12},{1,17},{... | collective-permute-start | bytes 528392 | tf_op jit(solution)/shard_map/ppermute | solution.py:110
Sparse Core Ops, SparseCore 0:
  109.3 55.8 all-gather.1
  204.2 43.7 reduce-scatter.3
  250.3 22.2 reduce-scatter.7
  276.1 33.0 reduce-scatter.5
